TPU v7x, 32 devices: a whole 2x2x4 slice. The times are simulated.
32 devices in a mesh: shot: 2 (over y), row: 4 (over x, core), freq: 4 (over z).
Axes of the slice: x: 2, y: 2, z: 4, core: 2. Of those that a mesh axis runs over, the one named last changes fastest.
Arguments:
- source_field: float32 [2, 8, 1024, 1024], P(None, ('shot', 'freq'), 'row'), parts along dimension 1, may hold values from -6 to 6
- receiver_field: float32 [2, 8, 1024, 1024], P(None, ('shot', 'freq'), 'row'), parts along dimension 1, may hold values from -6 to 6
- slowness: float32 [4, 1024, 1024], P('freq', 'row'), may hold values from 0.22 to 0.67
- owner: int32 [4], replicated, may hold values from 0 to 3, each once
- freq_index: int32 [8], P(('shot', 'freq')), parts along dimension 0, may hold values from 0 to 3, each once
Outputs:
- source_out: float32 [2, 8, 1024, 1024], P(None, ('shot', 'freq'), 'row'), parts along dimension 1
- receiver_out: float32 [2, 8, 1024, 1024], P(None, ('shot', 'freq'), 'row'), parts along dimension 1
- image: float32 [4, 1024, 1024], P('shot', 'row', 'freq'), parts along dimension 0
There are 2 independent parts, one for each index of `shot`. A program takes and returns all parts, laid end to end along the dimension named above; an argument that names none is the same for every part. Nothing has to cross between parts.
All inputs are finite; a program needn't handle non-finite values.
Results may differ from a plain program's by a relative error of at most 0.00022.
Values sent between devices are 32-bit elements; how exact they have to be, the bound alone decides.
A program may use at most 128 MiB of HBM per device.

v0:
```python
import math
import jax
import jax.numpy as jnp
from jax import lax
from jax.sharding import PartitionSpec as P

NZ = 2
dz_km = 0.01
dx_km = 0.0125
ref_slow = 0.5
base_hertz = 3.0
step_hertz = 4.0
taper = 0.5


def spread(value, axis, source):
    kept = jnp.where(lax.axis_index(axis) == source, value, 0).astype(value.dtype)
    return lax.psum(kept, axis)


def split_length(length):
    return length // 128


def angle_table(count_a, count_b, modulus, sign):
    left = jnp.arange(count_a, dtype=jnp.int32)[:, None]
    right = jnp.arange(count_b, dtype=jnp.int32)[None, :]
    turns = (left * right % modulus).astype(jnp.float32) * (2.0 * math.pi / modulus)
    return (jnp.cos(turns), sign * jnp.sin(turns))


def contract(form, left, right):
    return jnp.einsum(form, left, right, precision=lax.Precision.HIGHEST)


def transform_pair(real_part, imag_part, sign, last):
    length = real_part.shape[2] if last else real_part.shape[1]
    first = split_length(length)
    second = length // first
    cos_a, sin_a = angle_table(first, first, first, sign)
    cos_b, sin_b = angle_table(second, second, second, sign)
    twist_c, twist_s = angle_table(first, second, length, sign)
    if last:
        shape = (real_part.shape[0], real_part.shape[1], first, second)
        form_one = "fajb,jk->fakb"
        form_two = "fakb,bm->famk"
    else:
        shape = (real_part.shape[0], first, second, real_part.shape[2])
        form_one = "fjbq,jk->fkbq"
        form_two = "fkbq,bm->fmkq"
        twist_c = twist_c[:, :, None]
        twist_s = twist_s[:, :, None]
    x_re = real_part.reshape(shape)
    x_im = imag_part.reshape(shape)
    y_re = contract(form_one, x_re, cos_a) - contract(form_one, x_im, sin_a)
    y_im = contract(form_one, x_im, cos_a) + contract(form_one, x_re, sin_a)
    z_re = y_re * twist_c - y_im * twist_s
    z_im = y_im * twist_c + y_re * twist_s
    out_re = contract(form_two, z_re, cos_b) - contract(form_two, z_im, sin_b)
    out_im = contract(form_two, z_im, cos_b) + contract(form_two, z_re, sin_b)
    return (out_re.reshape(real_part.shape), out_im.reshape(real_part.shape))


def transform(block, sign, last):
    count = block.shape[0]
    freqs = block.shape[2]
    plane = block.shape[3:]
    real_part = block[:, 0].reshape((count * freqs,) + plane)
    imag_part = block[:, 1].reshape((count * freqs,) + plane)
    out_re, out_im = transform_pair(real_part, imag_part, sign, last)
    shape = (count, freqs) + plane
    return jnp.stack([out_re.reshape(shape), out_im.reshape(shape)], axis=1)


def wavenumbers(length, start, count):
    index = start + jnp.arange(count, dtype=jnp.int32)
    signed = jnp.where(index * 2 < length, index, index - length)
    return signed.astype(jnp.float32) * (2.0 * math.pi / (length * dx_km))


def rotate(block, cos_v, sin_v):
    real_part = block[:, 0]
    imag_part = block[:, 1]
    return jnp.stack(
        [real_part * cos_v - imag_part * sin_v, imag_part * cos_v + real_part * sin_v], axis=1
    )


def shift_phase(block, omega, kx_part, ky_part, total):
    square = kx_part[:, None] ** 2 + ky_part[None, :] ** 2
    kmax = math.pi / dx_km
    damp = jnp.exp(-taper * square / (kmax * kmax)) / total
    ws0 = omega[:, None, None] * ref_slow
    vertical = ws0 - 0.5 * square[None] / ws0
    cos_v = jnp.cos(dz_km * vertical) * damp
    sin_v = jnp.sin(dz_km * vertical) * damp
    return rotate(block, cos_v, sin_v)


def correct(block, slab, omega):
    theta = omega[:, None, None] * (slab[None] - ref_slow) * dz_km
    return rotate(block, jnp.cos(theta), jnp.sin(theta))


def image_term(block):
    return jnp.sum(block[0, 0] * block[1, 0] - block[0, 1] * block[1, 1], axis=0)


def body(source_field, receiver_field, slowness, owner, freq_index):
    rows = source_field.shape[2]
    width = source_field.shape[3]
    row_count = lax.axis_size("row")
    height = rows * row_count
    cols = width // row_count
    place = lax.axis_index("row")
    omega = 2.0 * math.pi * (base_hertz + step_hertz * freq_index.astype(jnp.float32))
    mirrored = jnp.stack([receiver_field[0], -receiver_field[1]])
    fields = jnp.stack([source_field, mirrored])
    kx_all = wavenumbers(height, 0, height)
    ky_own = wavenumbers(width, place * cols, cols)
    total = float(height * width)
    slab_dev = slowness.shape[0]
    images = []
    for depth in range(NZ):
        chosen = owner[depth]
        held = spread(slowness, "freq", chosen // slab_dev)
        slab = lax.dynamic_index_in_dim(held, chosen % slab_dev, 0, keepdims=False)
        fields = transform(fields, -1.0, True)
        fields = lax.all_to_all(fields, "row", split_axis=4, concat_axis=3, tiled=True)
        items = fields
        items = transform(items, -1.0, False)
        items = shift_phase(items, omega, kx_all, ky_own, total)
        fields = transform(items, 1.0, False)
        fields = lax.all_to_all(fields, "row", split_axis=3, concat_axis=4, tiled=True)
        fields = transform(fields, 1.0, True)
        fields = correct(fields, slab, omega)
        images.append(image_term(fields))
    parts = [lax.psum_scatter(term, "freq", scatter_dimension=1, tiled=True) for term in images]
    image = jnp.stack(parts)
    source_out = fields[0]
    receiver_out = jnp.stack([fields[1, 0], -fields[1, 1]])
    return (source_out, receiver_out, image)


def solution(mesh):
    in_specs = (
        P(None, ("shot", "freq"), "row", None),
        P(None, ("shot", "freq"), "row", None),
        P("freq", "row", None),
        P(),
        P(("shot", "freq")),
    )
    out_specs = (
        P(None, ("shot", "freq"), "row", None),
        P(None, ("shot", "freq"), "row", None),
        P("shot", "row", "freq"),
    )
    return jax.shard_map(body, mesh=mesh, in_specs=in_specs, out_specs=out_specs, check_vma=False)
```

profile of v0, /device:TPU:0, one launch (start us, length us, event | category | flops | bytes accessed | tf_op | source)
XLA Modules:
  0.0 596.2 jit_solution(643073891319918496)
XLA Ops:
  32.7 5.4 copy.346
  38.1 4.9 all-to-all-start
  44.0 4.0 fusion.186
  48.1 43.7 %all-to-all-done = f32[2,2,1,256,1024]{3,0,2,1,4:T(2,128)} async-done(((f32[2,2,1,256,1024]{3,0,2,1,4:T(2,128)}), f32[2,2,1,256,1024]{3,0,2,1,4:T(2,128)}, u32[]{:S(2)}, u32[]{:S(2)}) %all-to-all-start) | async-done | bytes 4194336 | tf_op jit(solution)/shard_map/all_to_all | solution.py:129
  91.8 5.0 copy.347
  96.7 5.4 copy.348
  104.7 2.9 fusion.104
  110.5 2.9 fusion.118
  113.4 3.8 subtract_bitcast_fusion.13
  131.0 2.9 fusion.88
  133.9 2.9 fusion.86
  136.8 3.0 fusion.124
  139.8 3.9 subtract_bitcast_fusion.11
  157.1 5.2 copy.372
  162.4 5.0 all-to-all-start.1
  171.0 90.0 %all-reduce.3.cloned.1.call-done = (f32[1,256,1024]{2,1,0:T(8,128)}, f32[1,256,1024]{2,1,0:T(8,128)}) async-done(((f32[1,256,1024]{2,1,0:T(8,128)}, f32[1,256,1024]{2,1,0:T(8,128)}), (f32[1,256,1024]{2,1,0:T(8,128)}, f32[1,256,1024]{2,1,0:T(8,128)})) %all-reduce.3.cloned.1.call-update) | async-done | bytes 2097168 | tf_op jit(solution)/shard_map/psum | solution.py:18
  260.9 4.7 fusion.192
  268.6 5.0 copy.373
  273.6 5.3 copy.374
  278.9 4.6 fusion.663
  285.6 3.2 fusion.318
  312.5 2.9 copy.386
  315.4 4.8 fusion.314
  320.2 3.1 copy.385
  323.3 3.6 fusion.316
  343.5 3.2 copy.395
  346.8 50.7 %all_to_all.72 = f32[2,2,1,256,1024]{3,0,2,1,4:T(2,128)S(1)} all-to-all(f32[2,2,1,256,1024]{3,0,2,1,4:T(2,128)S(1)} %copy.395), channel_id=1, replica_groups=mesh['shot'=2,'row'=4,'freq'=4] {'row'}, dimensions={4} | all-to-all | bytes 8388608 | tf_op jit(solution)/shard_map/all_to_all | solution.py:129
  400.3 5.7 copy.397
  408.5 2.9 fusion.56
  414.3 2.9 fusion.130
  417.2 3.6 subtract_bitcast_fusion.5
  434.6 2.9 fusion.40
  437.5 2.9 fusion.38
  440.3 3.0 fusion.136
  443.4 4.0 subtract_bitcast_fusion.3
  460.8 5.2 copy.418
  466.0 4.9 all-to-all-start.3
  474.9 5.7 cosine_bitcast_fusion
  484.7 4.7 fusion.10
  490.7 28.5 %all-to-all-done.3 = f32[2,2,1,1024,256]{4,0,2,1,3:T(2,128)} async-done(((f32[2,2,1,1024,256]{4,0,2,1,3:T(2,128)}), f32[2,2,1,1024,256]{4,0,2,1,3:T(2,128)}, u32[]{:S(2)}, u32[]{:S(2)}) %all-to-all-start.3) | async-done | bytes 4194336 | tf_op jit(solution)/shard_map/all_to_all | solution.py:134
  519.2 5.0 copy.419
  524.2 5.3 copy.420
  529.4 4.6 fusion.661
  536.1 3.2 fusion.306
  562.1 3.0 pad_maximum_fusion.6
  565.1 3.0 copy.444
  568.1 4.3 fusion.14
  574.3 13.1 %reduce-scatter.5.cloned.1.call-done = f32[256,256]{0,1:T(8,128)} async-done(((f32[256,1024]{0,1:T(8,128)}), f32[256,256]{0,1:T(8,128)}) %reduce-scatter.5.cloned.1.call-update) | async-done | bytes 262160 | tf_op jit(solution)/shard_map/reduce_scatter | solution.py:138
  (153 shorter events, 178.6 us)
Async XLA Ops:
  8.9 1.6 copy-start.19
  38.1 53.7 %all-to-all-start = ((f32[2,2,1,256,1024]{3,0,2,1,4:T(2,128)}), f32[2,2,1,256,1024]{3,0,2,1,4:T(2,128)}, u32[]{:S(2)}, u32[]{:S(2)}) async-start(f32[2,2,1,256,1024]{3,0,2,1,4:T(2,128)} %copy.346), calls=%async_computation | async-start | bytes 8388608 | tf_op jit(solution)/shard_map/all_to_all | solution.py:129
  48.1 82.2 %copy-start.8 = (f32[8,128,256]{2,1,0:T(8,128)}, f32[8,128,256]{2,1,0:T(8,128)S(1)}, u32[]{:S(2)}) copy-start(f32[8,128,256]{2,1,0:T(8,128)S(1)} %get-tuple-element.67) | copy-start | bytes 3145732
  162.4 5.1 copy-start.21
  162.4 7.0 %copy-start.20 = (f32[1,256,1024]{2,1,0:T(8,128)S(1)}, f32[1,256,1024]{2,1,0:T(8,128)}, u32[]{:S(2)}) copy-start(f32[1,256,1024]{2,1,0:T(8,128)} %param.7) | copy-start | bytes 3145732
  162.4 106.2 %all-to-all-start.1 = ((f32[2,2,1,1024,256]{4,0,2,1,3:T(2,128)}), f32[2,2,1,1024,256]{4,0,2,1,3:T(2,128)}, u32[]{:S(2)}, u32[]{:S(2)}) async-start(f32[2,2,1,1024,256]{4,0,2,1,3:T(2,128)} %copy.372), calls=%async_computation.1 | async-start | bytes 8388608 | tf_op jit(solution)/shard_map/all_to_all | solution.py:134
  167.4 93.5 %all-reduce.3.cloned.1.call-start = ((), (), s32[]{:S(2)}) async-start(), calls=%async_computation.8 | async-start | bytes 4194304 | tf_op jit(solution)/shard_map/psum | solution.py:18
  265.7 2.9 copy-start.11
  265.7 2.9 copy-start.13
  285.6 3.2 copy-start.6
  291.1 1.9 copy-start.14
  293.0 2.0 copy-start.7
  307.1 1.3 copy-start.1
  308.4 1.2 copy-start.17
  308.4 1.5 copy-start.18
  323.2 3.6 copy-start.2
  323.3 3.6 copy-start.15
  326.9 2.0 copy-start.5
  432.6 1.2 copy-start.9
  466.0 53.1 %all-to-all-start.3 = ((f32[2,2,1,1024,256]{4,0,2,1,3:T(2,128)}), f32[2,2,1,1024,256]{4,0,2,1,3:T(2,128)}, u32[]{:S(2)}, u32[]{:S(2)}) async-start(f32[2,2,1,1024,256]{4,0,2,1,3:T(2,128)} %copy.418), calls=%async_computation.3 | async-start | bytes 8388608 | tf_op jit(solution)/shard_map/all_to_all | solution.py:134
  470.9 2.7 copy-start.12
  470.9 103.4 %reduce-scatter.3.cloned.1.call-start = ((), (), s32[]{:S(2)}) async-start(), calls=%async_computation.6 | async-start | bytes 1310720 | tf_op jit(solution)/shard_map/reduce_scatter | solution.py:138
  490.7 96.8 %reduce-scatter.5.cloned.1.call-start = ((), (), s32[]{:S(2)}) async-start(), calls=%async_computation.7 | async-start | bytes 1310720 | tf_op jit(solution)/shard_map/reduce_scatter | solution.py:138
  536.1 3.2 copy-start.3
  541.8 1.9 copy-start.16
  543.7 2.0 copy-start.4
  555.2 2.3 copy-start.10
  557.5 2.5 copy-start
Sparse Core Ops, SparseCore 0:
  171.2 89.6 all-reduce.2
  490.8 26.5 reduce-scatter.2
  562.2 25.1 reduce-scatter.4
where the time goes:
time: 606 us; the launch traced here: 596 us
  waiting for transfers between devices  175 us (29%)
  matrix products  170 us (28%)
  local copies, waits for them, and re-layouts  125 us (21%)
  blocking collectives  50.7 us (8%)
  other arithmetic  42.9 us (7%)
  between operations  17.4 us (3%)
  starting transfers between devices  14.9 us (2%)
    dot_general x64, matrix products, contract(): return jnp.einsum(form, left, right, precision=lax.Precision.HIGHEST)  170 us
    psum x1, waiting for transfers between devices, spread(): return lax.psum(kept, axis)  90 us
    all_to_all x1, blocking collectives, body(): lax.all_to_all(fields, 'row', split_axis=4, concat_axis=3, tiled=True)  50.7 us
    all_to_all x1, waiting for transfers between devices, body(): lax.all_to_all(fields, 'row', split_axis=4, concat_axis=3, tiled=True)  43.7 us
    all_to_all x2, waiting for transfers between devices, body(): lax.all_to_all(fields, 'row', split_axis=3, concat_axis=4, tiled=True)  28.5 us
    all_to_all x4, local copies, waits for them, and re-layouts, body(): lax.all_to_all(fields, 'row', split_axis=3, concat_axis=4, tiled=True)  20.5 us
    another operation x4, local copies, waits for them, and re-layouts, transform(): return jnp.stack([out_re.reshape(shape), out_im.reshape(shape)], axis=1)  19.1 us
    all_to_all x4, local copies, waits for them, and re-layouts, body(): lax.all_to_all(fields, 'row', split_axis=4, concat_axis=3, tiled=True)  18.9 us
  transfers between devices with their start and end apart: 6, of which 4 were waited for; matrix products, arithmetic and copies ran while one was open for 15% of the time, Pallas kernels for 0%

commit v1 on v0

--- a/solution.py
+++ b/solution.py
@@ -11,6 +11,43 @@
 base_hertz = 3.0
 step_hertz = 4.0
 taper = 0.5
+
+
+def solve_the_body(x_local, along_dim, tile_in):
+    extra = x_local.shape
+    tall = x_local.reshape(
+        *extra[:along_dim], tile_in, extra[along_dim] // tile_in, *extra[along_dim + 1 :]
+    )
+    new = jnp.moveaxis(tall, along_dim, 0)
+    return new
+
+
+def find_steps_all(inputs, dimension_no):
+    inputs = jnp.moveaxis(inputs, 0, dimension_no)
+    base_arr = inputs.shape
+    row_out = inputs.reshape(
+        *base_arr[:dimension_no],
+        base_arr[dimension_no] * base_arr[dimension_no + 1],
+        *base_arr[dimension_no + 2 :]
+    )
+    return row_out
+
+
+def things_solve(my_data, mesh_ax, original, local_values):
+    mat_out = lax.axis_size(mesh_ax)
+    mid_arr, view_out = (mat_out, lax.axis_index(mesh_ax))
+    small = solve_the_body(my_data, original, mid_arr)
+    pool = [small[view_out]]
+    for tick in range(1, mid_arr):
+        v_now = small[(view_out + tick) % mid_arr]
+        seen_now = lax.ppermute(
+            v_now, mesh_ax, [(dd, (dd + tick) % mid_arr) for dd in range(mid_arr)]
+        )
+        pool.append(seen_now)
+    response = jnp.stack(pool, 0)
+    small = response[(view_out - jnp.arange(mid_arr)) % mid_arr]
+    built = find_steps_all(small, local_values)
+    return built
 
 
 def spread(value, axis, source):
@@ -131,7 +168,7 @@
         items = transform(items, -1.0, False)
         items = shift_phase(items, omega, kx_all, ky_own, total)
         fields = transform(items, 1.0, False)
-        fields = lax.all_to_all(fields, "row", split_axis=3, concat_axis=4, tiled=True)
+        fields = things_solve(fields, "row", 3, 4)
         fields = transform(fields, 1.0, True)
         fields = correct(fields, slab, omega)
         images.append(image_term(fields))

time: 606 us -> 553 us (0.913)
  blocking collectives: 50.7 us -> 0 us
  waiting for transfers between devices: 175 us -> 162 us
  other arithmetic: 42.9 us -> 52.3 us
    psum x1, waiting for transfers between devices: 90 us -> 0.02 us  [spread(): return lax.psum(kept, axis)]
    ppermute x0 -> x6, waiting for transfers between devices: none -> 59.3 us  [things_solve(): lax.ppermute(v_now, mesh_ax, [(dd, (dd + tick) % mid_arr) for dd in range...]
    all_to_all x1 -> x0, blocking collectives: 50.7 us -> none  [body(): lax.all_to_all(fields, 'row', split_axis=4, concat_axis=3, tiled=True)]
    all_to_all x1 -> x2, waiting for transfers between devices: 43.7 us -> 83.3 us  [body(): lax.all_to_all(fields, 'row', split_axis=4, concat_axis=3, tiled=True)]
    all_to_all x2 -> x0, waiting for transfers between devices: 28.5 us -> none  [body(): lax.all_to_all(fields, 'row', split_axis=3, concat_axis=4, tiled=True)]
    all_to_all x4 -> x0, local copies, waits for them, and re-layouts: 20.5 us -> none  [body(): lax.all_to_all(fields, 'row', split_axis=3, concat_axis=4, tiled=True)]
    transpose x0 -> x2, local copies, waits for them, and re-layouts: none -> 10.5 us  [find_steps_all(): inputs = jnp.moveaxis(inputs, 0, dimension_no)]
    gather x0 -> x2, local copies, waits for them, and re-layouts: none -> 10 us  [things_solve(): small = response[(view_out - jnp.arange(mid_arr)) % mid_arr]]
  transfers between devices with their start and end apart: 6 -> 11, of which waited for: 4 -> 9; matrix products, arithmetic and copies ran while one was open for 15% -> 31% of each run, Pallas kernels for 0% -> 0%
where the time goes in v1:
time: 553 us; the launch traced here: 543 us
  matrix products  170 us (31%)
  waiting for transfers between devices  162 us (29%)
  local copies, waits for them, and re-layouts  128 us (23%)
  other arithmetic  52.3 us (9%)
  between operations  17.4 us (3%)
  starting transfers between devices  13.5 us (2%)
    dot_general x64, matrix products, contract(): return jnp.einsum(form, left, right, precision=lax.Precision.HIGHEST)  170 us
    all_to_all x2, waiting for transfers between devices, body(): lax.all_to_all(fields, 'row', split_axis=4, concat_axis=3, tiled=True)  83.3 us
    ppermute x6, waiting for transfers between devices, things_solve(): lax.ppermute(v_now, mesh_ax, [(dd, (dd + tick) % mid_arr) for dd in range...  59.3 us
    all_to_all x4, local copies, waits for them, and re-layouts, body(): lax.all_to_all(fields, 'row', split_axis=4, concat_axis=3, tiled=True)  21 us
    reduce_scatter x2, waiting for transfers between devices, body(): lax.psum_scatter(term, 'freq', scatter_dimension=1, tiled=True)  19.2 us
    sub x5, other arithmetic, rotate(): real_part * cos_v - imag_part * sin_v  12.8 us
  transfers between devices with their start and end apart: 11, of which 9 were waited for; matrix products, arithmetic and copies ran while one was open for 31% of the time, Pallas kernels for 0%

profile of v1, /device:TPU:0, one launch (start us, length us, event | category | flops | bytes accessed | tf_op | source)
XLA Modules:
  0.0 542.8 jit_solution(14480310383921981788)
XLA Ops:
  32.7 5.4 copy.362
  38.1 5.0 all-to-all-start
  47.7 4.0 fusion.186
  51.8 40.1 %all-to-all-done = f32[2,2,1,256,1024]{3,0,2,1,4:T(2,128)} async-done(((f32[2,2,1,256,1024]{3,0,2,1,4:T(2,128)}), f32[2,2,1,256,1024]{3,0,2,1,4:T(2,128)}, u32[]{:S(2)}, u32[]{:S(2)}) %all-to-all-start) | async-done | bytes 4194336 | tf_op jit(solution)/shard_map/all_to_all | solution.py:166
  91.9 5.0 copy.363
  96.9 5.6 %copy.364 = f32[2,2,1,4,256,256]{5,4,3,1,0,2:T(8,128)} copy(f32[2,2,1,4,256,256]{4,5,3,1,0,2:T(8,128)} %bitcast.484) | data formatting | bytes 8388608 | tf_op jit(solution)/shard_map/all_to_all | solution.py:166
  110.8 2.9 fusion.118
  113.7 3.8 subtract_bitcast_fusion.13
  137.1 3.0 fusion.124
  140.1 3.7 subtract_bitcast_fusion.11
  152.9 3.0 subtract_bitcast_fusion.10
  163.5 4.7 fusion.200
  172.5 11.1 %collective-permute-done = f32[2,2,1,256,256]{4,3,1,0,2:T(8,128)} collective-permute-done((f32[2,2,1,256,256]{4,3,1,0,2:T(8,128)}, f32[2,2,1,256,256]{4,3,1,0,2:T(8,128)}, u32[]{:S(2)}, u32[]{:S(2)}) %collective-permute-start) | collective-permute-done | bytes 1048608 | tf_op jit(solution)/shard_map/ppermute | solution.py:43
  183.6 3.5 collective-permute-done.1
  187.1 18.1 %collective-permute-done.2 = f32[2,2,1,256,256]{4,3,1,0,2:T(8,128)} collective-permute-done((f32[2,2,1,256,256]{4,3,1,0,2:T(8,128)}, f32[2,2,1,256,256]{4,3,1,0,2:T(8,128)}, u32[]{:S(2)}, u32[]{:S(2)}) %collective-permute-start.2) | collective-permute-done | bytes 1048608 | tf_op jit(solution)/shard_map/ppermute | solution.py:43
  205.2 4.2 maximum_bitcast_fusion
  209.4 5.0 gather_fusion
  214.4 5.3 copy.392
  219.7 4.6 fusion.641
  226.4 3.2 fusion.326
  253.1 2.9 copy.404
  256.0 4.8 fusion.322
  260.8 3.3 copy.403
  264.1 3.6 fusion.324
  284.4 5.2 copy.413
  289.6 4.9 all-to-all-start.1
  299.7 43.1 %all-to-all-done.1 = f32[2,2,1,256,1024]{3,0,2,1,4:T(2,128)} async-done(((f32[2,2,1,256,1024]{3,0,2,1,4:T(2,128)}), f32[2,2,1,256,1024]{3,0,2,1,4:T(2,128)}, u32[]{:S(2)}, u32[]{:S(2)}) %all-to-all-start.1) | async-done | bytes 4194336 | tf_op jit(solution)/shard_map/all_to_all | solution.py:166
  342.8 5.0 copy.414
  347.8 5.4 %copy.415 = f32[2,2,1,4,256,256]{5,4,3,1,0,2:T(8,128)} copy(f32[2,2,1,4,256,256]{4,5,3,1,0,2:T(8,128)} %bitcast.486) | data formatting | bytes 8388608 | tf_op jit(solution)/shard_map/all_to_all | solution.py:166
  361.6 2.9 fusion.130
  364.5 3.8 subtract_bitcast_fusion.5
  382.1 2.9 fusion.40
  387.8 3.0 fusion.136
  390.8 3.7 subtract_bitcast_fusion.3
  403.7 3.0 subtract_bitcast_fusion.2
  414.2 4.6 cosine_bitcast_fusion
  422.9 4.7 fusion.10
  429.0 5.4 collective-permute-done.3
  434.4 3.4 collective-permute-done.4
  437.8 17.8 %collective-permute-done.5 = f32[2,2,1,256,256]{4,3,1,0,2:T(8,128)} collective-permute-done((f32[2,2,1,256,256]{4,3,1,0,2:T(8,128)}, f32[2,2,1,256,256]{4,3,1,0,2:T(8,128)}, u32[]{:S(2)}, u32[]{:S(2)}) %collective-permute-start.5) | collective-permute-done | bytes 1048608 | tf_op jit(solution)/shard_map/ppermute | solution.py:43
  455.6 4.3 maximum_bitcast_fusion.1
  459.9 5.0 gather_fusion.1
  464.9 5.3 copy.440
  470.1 4.6 fusion.639
  476.9 3.2 fusion.314
  502.6 3.0 pad_maximum_fusion.4
  508.5 4.3 fusion.14
  514.8 19.2 %reduce-scatter.5.cloned.1.call-done = f32[256,256]{0,1:T(8,128)} async-done(((f32[256,1024]{0,1:T(8,128)}), f32[256,256]{0,1:T(8,128)}) %reduce-scatter.5.cloned.1.call-update) | async-done | bytes 262160 | tf_op jit(solution)/shard_map/reduce_scatter | solution.py:175
  (174 shorter events, 201.5 us)
Async XLA Ops:
  9.0 1.6 copy-start.19
  38.1 5.1 copy-start.22
  38.1 7.0 %copy-start.20 = (f32[1,256,1024]{2,1,0:T(8,128)S(1)}, f32[1,256,1024]{2,1,0:T(8,128)}, u32[]{:S(2)}) copy-start(f32[1,256,1024]{2,1,0:T(8,128)} %param.7) | copy-start | bytes 3145732
  38.1 53.8 %all-to-all-start = ((f32[2,2,1,256,1024]{3,0,2,1,4:T(2,128)}), f32[2,2,1,256,1024]{3,0,2,1,4:T(2,128)}, u32[]{:S(2)}, u32[]{:S(2)}) async-start(f32[2,2,1,256,1024]{3,0,2,1,4:T(2,128)} %copy.362), calls=%async_computation | async-start | bytes 8388608 | tf_op jit(solution)/shard_map/all_to_all | solution.py:166
  43.1 120.4 %all-reduce.3.cloned.1.call-start = ((), (), s32[]{:S(2)}) async-start(), calls=%async_computation.6 | async-start | bytes 4194304 | tf_op jit(solution)/shard_map/psum | solution.py:55
  51.8 78.8 %copy-start.8 = (f32[8,128,256]{2,1,0:T(8,128)}, f32[8,128,256]{2,1,0:T(8,128)S(1)}, u32[]{:S(2)}) copy-start(f32[8,128,256]{2,1,0:T(8,128)S(1)} %get-tuple-element.75) | copy-start | bytes 3145732
  159.6 24.0 %collective-permute-start = (f32[2,2,1,256,256]{4,3,1,0,2:T(8,128)}, f32[2,2,1,256,256]{4,3,1,0,2:T(8,128)}, u32[]{:S(2)}, u32[]{:S(2)}) collective-permute-start(f32[2,2,1,256,256]{4,3,1,0,2:T(8,128)} %bitcast.451), channel_id=1, source_target_pairs={{0,4},{4,8},{8,12},{12,0},{1,5},{5,9},{9,13},{13,1},{2,6},{6,10},{... | collective-permute-start | bytes 3145736 | tf_op jit(solution)/shard_map/ppermute | solution.py:43
  160.7 26.4 %collective-permute-start.1 = (f32[2,2,1,256,256]{4,3,1,0,2:T(8,128)}, f32[2,2,1,256,256]{4,3,1,0,2:T(8,128)}, u32[]{:S(2)}, u32[]{:S(2)}) collective-permute-start(f32[2,2,1,256,256]{4,3,1,0,2:T(8,128)} %bitcast.450), channel_id=1, source_target_pairs={{0,8},{4,12},{8,0},{12,4},{1,9},{5,13},{9,1},{13,5},{2,10},{6,14},... | collective-permute-start | bytes 3145736 | tf_op jit(solution)/shard_map/ppermute | solution.py:43
  161.7 43.4 %collective-permute-start.2 = (f32[2,2,1,256,256]{4,3,1,0,2:T(8,128)}, f32[2,2,1,256,256]{4,3,1,0,2:T(8,128)}, u32[]{:S(2)}, u32[]{:S(2)}) collective-permute-start(f32[2,2,1,256,256]{4,3,1,0,2:T(8,128)} %bitcast.449), channel_id=1, source_target_pairs={{0,12},{4,0},{8,4},{12,8},{1,13},{5,1},{9,5},{13,9},{2,14},{6,2},{... | collective-permute-start | bytes 3145736 | tf_op jit(solution)/shard_map/ppermute | solution.py:43
  168.3 2.9 copy-start.11
  168.3 2.9 copy-start.12
  226.4 3.2 copy-start.6
  231.9 1.9 copy-start.13
  233.7 2.0 copy-start.7
  247.7 1.3 copy-start.1
  249.0 1.2 copy-start.16
  249.0 1.5 copy-start.17
  264.1 3.6 copy-start.2
  264.1 3.6 copy-start.14
  267.7 2.0 copy-start.5
  289.6 53.2 %all-to-all-start.1 = ((f32[2,2,1,256,1024]{3,0,2,1,4:T(2,128)}), f32[2,2,1,256,1024]{3,0,2,1,4:T(2,128)}, u32[]{:S(2)}, u32[]{:S(2)}) async-start(f32[2,2,1,256,1024]{3,0,2,1,4:T(2,128)} %copy.413), calls=%async_computation.1 | async-start | bytes 8388608 | tf_op jit(solution)/shard_map/all_to_all | solution.py:166
  294.5 220.3 %reduce-scatter.3.cloned.1.call-start = ((), (), s32[]{:S(2)}) async-start(), calls=%async_computation.4 | async-start | bytes 1310720 | tf_op jit(solution)/shard_map/reduce_scatter | solution.py:175
  380.1 1.2 copy-start.9
  410.3 24.1 %collective-permute-start.3 = (f32[2,2,1,256,256]{4,3,1,0,2:T(8,128)}, f32[2,2,1,256,256]{4,3,1,0,2:T(8,128)}, u32[]{:S(2)}, u32[]{:S(2)}) collective-permute-start(f32[2,2,1,256,256]{4,3,1,0,2:T(8,128)} %bitcast.447), channel_id=1, source_target_pairs={{0,4},{4,8},{8,12},{12,0},{1,5},{5,9},{9,13},{13,1},{2,6},{6,10},{... | collective-permute-start | bytes 3145736 | tf_op jit(solution)/shard_map/ppermute | solution.py:43
  410.3 3.8 copy-start.21
  411.4 26.4 %collective-permute-start.4 = (f32[2,2,1,256,256]{4,3,1,0,2:T(8,128)}, f32[2,2,1,256,256]{4,3,1,0,2:T(8,128)}, u32[]{:S(2)}, u32[]{:S(2)}) collective-permute-start(f32[2,2,1,256,256]{4,3,1,0,2:T(8,128)} %bitcast.446), channel_id=1, source_target_pairs={{0,8},{4,12},{8,0},{12,4},{1,9},{5,13},{9,1},{13,5},{2,10},{6,14},... | collective-permute-start | bytes 3145736 | tf_op jit(solution)/shard_map/ppermute | solution.py:43
  412.7 42.9 %collective-permute-start.5 = (f32[2,2,1,256,256]{4,3,1,0,2:T(8,128)}, f32[2,2,1,256,256]{4,3,1,0,2:T(8,128)}, u32[]{:S(2)}, u32[]{:S(2)}) collective-permute-start(f32[2,2,1,256,256]{4,3,1,0,2:T(8,128)} %bitcast.445), channel_id=1, source_target_pairs={{0,12},{4,0},{8,4},{12,8},{1,13},{5,1},{9,5},{13,9},{2,14},{6,2},{... | collective-permute-start | bytes 3145736 | tf_op jit(solution)/shard_map/ppermute | solution.py:43
  427.5 1.3 copy-start.18
  428.8 105.1 %reduce-scatter.5.cloned.1.call-start = ((), (), s32[]{:S(2)}) async-start(), calls=%async_computation.5 | async-start | bytes 1310720 | tf_op jit(solution)/shard_map/reduce_scatter | solution.py:175
  476.9 3.2 copy-start.3
  482.3 1.9 copy-start.15
  484.2 2.0 copy-start.4
  495.8 2.3 copy-start.10
  498.1 2.5 copy-start
Sparse Core Ops, SparseCore 0:
  46.9 90.1 all-reduce.2
  428.9 29.9 reduce-scatter.2
  502.7 31.1 reduce-scatter.4
